TPU v7x, 512 devices: a whole 4x4x16 slice. The times are simulated.
512 devices in a mesh: row: 16 (over y_hi, x, core), col: 32 (over y_lo, z).
Axes of the slice: x: 4, y: 4 (y_hi: 2, y_lo: 2; y = y_hi * 2 + y_lo), z: 16, core: 2. Of those that a mesh axis runs over, the one named last changes fastest.
Arguments:
- inputs: bfloat16 [512, 8192], P('col', 'row'), may hold values from -6 to 6
- out_grad: bfloat16 [512, 8192], P('col', 'row'), may hold values from -0.8984375 to 0.8984375
- gate_pre: bfloat16 [512, 16384], P('row', 'col'), may hold values from -6 to 6
- up_pre: bfloat16 [512, 16384], P('row', 'col'), may hold values from -6 to 6
- gate_weight: bfloat16 [8192, 16384], P('row', 'col'), may hold values from -0.0625 to 0.0625
- up_weight: bfloat16 [8192, 16384], P('row', 'col'), may hold values from -0.0625 to 0.0625
- down_weight: bfloat16 [16384, 8192], P('col', 'row'), may hold values from -0.0625 to 0.0625
Outputs:
- input_grad: bfloat16 [512, 8192], P('col', 'row')
- gate_grad: bfloat16 [8192, 16384], P('row', 'col')
- up_grad: bfloat16 [8192, 16384], P('row', 'col')
- down_grad: bfloat16 [16384, 8192], P('col', 'row')
All inputs are finite; a program needn't handle non-finite values.
Results may differ from a plain program's by a relative error of at most 0.028.
Values may be sent and summed in bfloat16 or wider, within the bound.
No kernel may reach another device: no remote copies, remote signals or barrier semaphores. Data moves between devices by JAX's collectives and lax.ppermute only.
A program may use at most 64 MiB of HBM per device.

v0:
```python
import jax
import jax.numpy as jnp
from jax import lax
from jax.sharding import Mesh
from jax.sharding import PartitionSpec as P

COL = ("col_0", "col_1")
ROW = ("row_0", "row_1", "row_2")


def laid_out(blocks, dim):
    blocks = jnp.moveaxis(blocks, 0, dim)
    shape = blocks.shape
    return blocks.reshape(*shape[:dim], shape[dim] * shape[dim + 1], *shape[dim + 2 :])


def gather_in_order(array, axes, order):
    blocks = array
    for k in order:
        blocks = lax.all_gather(blocks, axes[k])
    done = order[::-1]
    back = [done.index(k) for k in range(len(axes))]
    blocks = blocks.transpose(*back, *range(len(axes), blocks.ndim))
    return blocks.reshape(-1, *array.shape)


def gathered_by_axis(array, axes, order, dim):
    return laid_out(gather_in_order(array, axes, order), dim)


def in_blocks(array, dim, peers):
    shape = array.shape
    blocks = array.reshape(*shape[:dim], peers, shape[dim] // peers, *shape[dim + 1 :])
    return jnp.moveaxis(blocks, dim, 0)


def sum_at_owner(array, axis, dim):
    blocks = in_blocks(array, dim, lax.axis_size(axis))
    arrived = lax.all_to_all(blocks, axis, split_axis=0, concat_axis=0, tiled=True)
    return arrived.astype(jnp.float32).sum(axis=0)


def sent_to_all(array, axis):
    peers = lax.axis_size(axis)
    return lax.all_to_all(
        jnp.broadcast_to(array[None], (peers, *array.shape)), axis, 0, 0, tiled=True
    )


def gathered_by_axis_2(array, axes, dim):
    far, near = axes
    blocks = sent_to_all(sent_to_all(array, far), near)
    return laid_out(blocks.swapaxes(0, 1).reshape(-1, *array.shape), dim)


def in_one_piece(arrays, axis, dim, along):
    ends, at = ([], 0)
    for a in arrays[:-1]:
        at += a.shape[along]
        ends.append(at)
    both = jnp.concatenate(arrays, axis=along)
    return tuple(jnp.split(gathered_by_axis_2(both, axis, dim), ends, axis=along))


def derivatives(gate_pre, up_pre, hidden_grad):
    gate_f32 = gate_pre.astype(jnp.float32)
    up_f32 = up_pre.astype(jnp.float32)
    sigmoid = 1.0 / (1.0 + jnp.exp(-gate_f32))
    activated = gate_f32 * sigmoid
    hidden = (activated * up_f32).astype(jnp.bfloat16)
    gate_delta = (hidden_grad * up_f32 * sigmoid * (1.0 + gate_f32 * (1.0 - sigmoid))).astype(
        jnp.bfloat16
    )
    up_delta = (hidden_grad * activated).astype(jnp.bfloat16)
    return (hidden, gate_delta, up_delta)


def per_device(inputs, out_grad, gate_pre, up_pre, gate_weight, up_weight, down_weight):
    by_cols = (((1,), (1,)), ((), ()))
    by_rows = (((0,), (0,)), ((), ()))
    all_inputs, all_grads = (
        gathered_by_axis(inputs, COL, (0, 1), 0),
        gathered_by_axis(out_grad, COL, (0, 1), 0),
    )
    hidden_share = sum_at_owner(
        lax.dot_general(all_grads, down_weight, by_cols, preferred_element_type=jnp.float32).astype(
            jnp.bfloat16
        ),
        ROW,
        0,
    )
    hidden_part, gate_part, up_part = derivatives(gate_pre, up_pre, hidden_share)
    hidden, gate_delta, up_delta = in_one_piece(
        (hidden_part, gate_part, up_part), (("row_0", "row_1"), "row_2"), 0, 1
    )
    down_grad = lax.dot_general(
        hidden, all_grads, by_rows, preferred_element_type=jnp.float32
    ).astype(jnp.bfloat16)
    gate_grad = lax.dot_general(
        all_inputs, gate_delta, by_rows, preferred_element_type=jnp.float32
    ).astype(jnp.bfloat16)
    up_grad = lax.dot_general(
        all_inputs, up_delta, by_rows, preferred_element_type=jnp.float32
    ).astype(jnp.bfloat16)
    gate_part_sum = lax.dot_general(
        gate_delta, gate_weight, by_cols, preferred_element_type=jnp.float32
    )
    input_grad = sum_at_owner(
        (
            gate_part_sum
            + lax.dot_general(up_delta, up_weight, by_cols, preferred_element_type=jnp.float32)
        ).astype(jnp.bfloat16),
        COL,
        0,
    ).astype(jnp.bfloat16)
    return (input_grad, gate_grad, up_grad, down_grad)


def solution(mesh):
    split = Mesh(
        mesh.devices.reshape(2, 4, 2, 2, 16), ("row_0", "row_1", "row_2", "col_0", "col_1")
    )
    in_specs = (
        P(COL, ROW),
        P(COL, ROW),
        P(ROW, COL),
        P(ROW, COL),
        P(ROW, COL),
        P(ROW, COL),
        P(COL, ROW),
    )
    out_specs = (P(COL, ROW), P(ROW, COL), P(ROW, COL), P(COL, ROW))
    return jax.shard_map(
        per_device, mesh=split, in_specs=in_specs, out_specs=out_specs, check_vma=False
    )
```

profile of v0, /device:TPU:8, one launch (start us, length us, event | category | flops | bytes accessed | tf_op | source)
XLA Modules:
  0.0 157.7 jit_solution(9997233606861488553)
XLA Ops:
  0.6 0.0 copy-start
  0.6 8.6 %all-gather = bf16[32,512]{1,0:T(8,128)(2,1)S(1)} all-gather(bf16[16,512]{1,0:T(8,128)(2,1)} %param.8), channel_id=2, replica_groups=mesh['row_0'=2,'row_1'=4,'row_2'=2,'col_0'=2,'col_1'=16] {'col_0'}, dimensions={0}, use_global_device_ids=true | all-gather | bytes 49152 | tf_op jit(solution)/shard_map/all_gather | solution.py:20
  9.2 34.7 %all-gather.1 = bf16[32,16,512]{2,1,0:T(8,128)(2,1)S(1)} all-gather(bf16[2,16,512]{2,1,0:T(8,128)(2,1)S(1)} %bitcast.38), channel_id=3, replica_groups=mesh['row_0'=2,'row_1'=4,'row_2'=2,'col_0'=2,'col_1'=16] {'col_1'}, dimensions={0}, use_global_device_ids=true | all-gather | bytes 557056 | tf_op jit(solution)/shard_map/all_gather | solution.py:20
  43.9 0.0 copy-done
  44.0 0.0 copy-start.4
  44.0 0.0 copy-start.5
  44.0 0.5 convolution_convert_fusion.3
  44.5 18.3 %all_to_all.20 = bf16[16,32,512]{2,1,0:T(8,128)(2,1)S(1)} all-to-all(bf16[16,32,512]{2,1,0:T(8,128)(2,1)S(1)} %bitcast.33), channel_id=1, replica_groups=mesh['row_0'=2,'row_1'=4,'row_2'=2,'col_0'=2,'col_1'=16] {'row_0','row_1..., dimensions={0} | all-to-all | bytes 1048576 | tf_op jit(solution)/shard_map/all_to_all | solution.py:39
  62.7 0.1 convert_reduce_fusion
  62.8 0.0 copy-done.4
  62.8 0.0 copy-done.5
  62.8 0.1 fusion.12
  62.9 0.1 broadcast_in_dim.4
  63.0 16.9 %all_to_all.21 = bf16[8,32,1536]{2,1,0:T(8,128)(2,1)S(1)} all-to-all(bf16[8,32,1536]{2,1,0:T(8,128)(2,1)S(1)} %broadcast_in_dim.4), channel_id=1, replica_groups=mesh['row_0'=2,'row_1'=4,'row_2'=2,'col_0'=2,'col_1'=16] {'row_0','row_1'}, dimensions={0} | all-to-all | bytes 1572864 | tf_op jit(solution)/shard_map/all_to_all | solution.py:45
  79.9 0.2 broadcast_in_dim.5
  80.0 5.0 %all_to_all.22 = bf16[2,8,32,1536]{3,2,1,0:T(8,128)(2,1)S(1)} all-to-all(bf16[2,8,32,1536]{3,2,1,0:T(8,128)(2,1)S(1)} %broadcast_in_dim.5), channel_id=1, replica_groups=mesh['row_0'=2,'row_1'=4,'row_2'=2,'col_0'=2,'col_1'=16] {'row_2'}, dimensions={0} | all-to-all | bytes 3145728 | tf_op jit(solution)/shard_map/all_to_all | solution.py:45
  85.0 0.0 copy-start.3
  85.0 0.1 copy.20
  85.1 0.0 copy-start.1
  85.2 0.9 copy-done.3
  86.1 0.5 fusion.7
  86.6 0.0 copy-done.1
  86.6 0.0 copy-start.6
  86.6 1.3 fusion
  87.8 8.2 %all-to-all-start.3 = ((bf16[32,16,512]{2,1,0:T(8,128)(2,1)}), bf16[32,16,512]{2,1,0:T(8,128)(2,1)S(1)}, u32[]{:S(2)}, u32[]{:S(2)}) async-start(bf16[32,16,512]{2,1,0:T(8,128)(2,1)} %bitcast.8), calls=%async_computation.3 | async-start | bytes 1048576 | tf_op jit(solution)/shard_map/all_to_all | solution.py:39
  96.1 0.0 copy-done.6
  96.1 4.4 %all-gather.2 = bf16[32,512]{1,0:T(8,128)(2,1)S(1)} all-gather(bf16[16,512]{1,0:T(8,128)(2,1)S(1)} %copy-done.6), channel_id=4, replica_groups=mesh['row_0'=2,'row_1'=4,'row_2'=2,'col_0'=2,'col_1'=16] {'col_0'}, dimensions={0}, use_global_device_ids=true | all-gather | bytes 49152 | tf_op jit(solution)/shard_map/all_gather | solution.py:20
  100.5 46.8 %all-gather.3 = bf16[32,16,512]{2,1,0:T(8,128)(2,1)S(1)} all-gather(bf16[2,16,512]{2,1,0:T(8,128)(2,1)S(1)} %bitcast.39), channel_id=5, replica_groups=mesh['row_0'=2,'row_1'=4,'row_2'=2,'col_0'=2,'col_1'=16] {'col_1'}, dimensions={0}, use_global_device_ids=true | all-gather | bytes 557056 | tf_op jit(solution)/shard_map/all_gather | solution.py:20
  147.3 0.0 copy-start.2
  147.3 0.8 copy-done.2
  148.1 1.3 fusion.1
  149.3 2.0 %copy.22 = bf16[512,512]{1,0:T(8,128)(2,1)} copy(bf16[512,512]{0,1:T(8,128)(2,1)} %fusion.1) | data formatting | bytes 1048576
  151.4 2.3 %fusion.2 = bf16[512,512]{0,1:T(8,128)(2,1)} fusion(bf16[512,512]{1,0:T(8,128)(2,1)} %bitcast.37, bf16[512,1536]{1,0:T(8,128)(2,1)S(1)} %bitcast.29), kind=kOutput, calls=%fused_computation.7 | convolution fusion | flops 268697600 | bytes 1572864 | tf_op jit(solution)/shard_map/dot_general | solution.py:102
  153.7 2.0 %copy.23 = bf16[512,512]{1,0:T(8,128)(2,1)} copy(bf16[512,512]{0,1:T(8,128)(2,1)} %fusion.2) | data formatting | bytes 1048576
  155.7 1.3 convolution_convert_fusion
  157.0 0.0 all-to-all-done.3
  157.0 0.7 reduce_sum.22
  (3 shorter events, 0.1 us)
Async XLA Ops:
  0.6 43.3 %copy-start = (bf16[512,512]{1,0:T(8,128)(2,1)S(1)}, bf16[512,512]{1,0:T(8,128)(2,1)}, u32[]{:S(2)}) copy-start(bf16[512,512]{1,0:T(8,128)(2,1)} %param.13) | copy-start | bytes 1572868
  44.0 18.8 %copy-start.4 = (bf16[32,512]{1,0:T(8,128)(2,1)S(1)}, bf16[32,512]{1,0:T(8,128)(2,1)}, u32[]{:S(2)}) copy-start(bf16[32,512]{1,0:T(8,128)(2,1)} %param.10) | copy-start | bytes 98308
  44.0 18.8 %copy-start.5 = (bf16[32,512]{1,0:T(8,128)(2,1)S(1)}, bf16[32,512]{1,0:T(8,128)(2,1)}, u32[]{:S(2)}) copy-start(bf16[32,512]{1,0:T(8,128)(2,1)} %param.9) | copy-start | bytes 98308
  85.0 1.0 copy-start.3
  85.1 1.4 copy-start.1
  86.6 9.5 %copy-start.6 = (bf16[16,512]{1,0:T(8,128)(2,1)S(1)}, bf16[16,512]{1,0:T(8,128)(2,1)}, u32[]{:S(2)}) copy-start(bf16[16,512]{1,0:T(8,128)(2,1)} %param.7) | copy-start | bytes 49156
  87.8 69.1 %all-to-all-start.3 = ((bf16[32,16,512]{2,1,0:T(8,128)(2,1)}), bf16[32,16,512]{2,1,0:T(8,128)(2,1)S(1)}, u32[]{:S(2)}, u32[]{:S(2)}) async-start(bf16[32,16,512]{2,1,0:T(8,128)(2,1)} %bitcast.8), calls=%async_computation.3 | async-start | bytes 1048576 | tf_op jit(solution)/shard_map/all_to_all | solution.py:39
  147.3 0.8 copy-start.2
where the time goes:
time: 158 us
  blocking collectives  135 us (85%)
  starting transfers between devices  8.2 us (5%)
  matrix products  7.01 us (4%)
  local copies, waits for them, and re-layouts  6.23 us (4%)
    all_gather x4, blocking collectives, gather_in_order(): blocks = lax.all_gather(blocks, axes[k])  94.4 us
    all_to_all x2, blocking collectives, sent_to_all(): lax.all_to_all(jnp.broadcast_to(array[None], (peers, *array.shape)), axis...  21.9 us
    all_to_all x1, blocking collectives, sum_at_owner(): lax.all_to_all(blocks, axis, split_axis=0, concat_axis=0, tiled=True)  18.3 us
    all_to_all x1, starting transfers between devices, sum_at_owner(): lax.all_to_all(blocks, axis, split_axis=0, concat_axis=0, tiled=True)  8.2 us
    unnamed x16, local copies, waits for them, and re-layouts  5.84 us
  transfers between devices with their start and end apart: 1, of which 0 were waited for; matrix products, arithmetic and copies ran while one was open for 6% of the time, Pallas kernels for 0%

commit v1 on v0

v1 whole, which is shorter than its diff:
```python
import jax
import jax.numpy as jnp
from jax import lax
from jax.sharding import Mesh
from jax.sharding import PartitionSpec as P

ROW = ("y_hi", "x_hi", "x_lo", "core")
PLANE = ("y_hi", "x_hi", "x_lo")
COL = ("y_lo", "z3", "z2", "z1", "z_lo")
NEAR = ("y_lo", "z_lo")
FAR = ("z3", "z2", "z1")


def product(x, y, contract):
    return lax.dot_general(
        x, y, (((contract,), (contract,)), ((), ())), preferred_element_type=jnp.float32
    )


def exchanged(blocks, axes):
    return lax.all_to_all(blocks, axes, 0, 0, tiled=True)


def sent_to_all(array, axes):
    peers = lax.axis_size(axes)
    return exchanged(jnp.broadcast_to(array[None], (peers, *array.shape)), axes)


def summed(blocks):
    return blocks.astype(jnp.float32).sum(axis=0)


def grads_gathered(array):
    tokens, width = array.shape
    far = sent_to_all(array, FAR)
    near = sent_to_all(far, NEAR)
    near = near.reshape(lax.axis_size("y_lo"), -1, far.shape[0], tokens, width).swapaxes(1, 2)
    return near.reshape(-1, width)


def doubled(array, axis, place):
    other = lax.ppermute(array, axis, ((0, 1), (1, 0)))
    second = lax.axis_index(axis) == 1
    return jnp.stack((jnp.where(second, other, array), jnp.where(second, array, other)), axis=place)


def inputs_gathered(inputs):
    blocks = doubled(inputs, "z3", 0)
    blocks = doubled(blocks, "z2", 1)
    blocks = doubled(blocks, "z1", 2)
    blocks = doubled(blocks, "z_lo", 3)
    blocks = doubled(blocks, "y_lo", 0)
    return blocks.reshape(-1, inputs.shape[1])


def pre_gathered(gate_pre, up_pre):
    blocks = jnp.stack((gate_pre, up_pre))
    blocks = doubled(blocks, "y_hi", 1)
    blocks = doubled(blocks, "x_hi", 2)
    blocks = doubled(blocks, "x_lo", 3)
    blocks = doubled(blocks, "core", 4)
    return blocks.reshape(2, -1, gate_pre.shape[1])


def hidden_sum(partial):
    peers = lax.axis_size(ROW)
    blocks = partial.reshape(peers, -1, partial.shape[1])
    share = summed(exchanged(blocks, ROW)).astype(jnp.bfloat16)
    plane = sent_to_all(share, PLANE)
    whole = lax.all_gather(plane, "core")
    return whole.swapaxes(0, 1).reshape(-1, share.shape[1])


def input_sum(partial, tokens):
    width = partial.shape[1]
    ys, zs, peers = lax.axis_size("y_lo"), lax.axis_size("z_lo"), lax.axis_size(FAR)
    blocks = partial.reshape(ys, peers, zs, tokens, width).swapaxes(1, 2)
    blocks = blocks.reshape(ys * zs, peers, tokens, width)
    near = summed(exchanged(blocks, NEAR)).astype(jnp.bfloat16)
    return summed(exchanged(near, FAR)).astype(jnp.bfloat16)


def per_device(inputs, out_grad, gate_pre, up_pre, gate_weight, up_weight, down_weight):
    bf16 = jnp.bfloat16
    all_grads = grads_gathered(out_grad)
    gate, up = pre_gathered(gate_pre, up_pre).astype(jnp.float32)
    all_inputs = inputs_gathered(inputs)
    hidden_grad = hidden_sum(product(all_grads, down_weight, 1).astype(bf16)).astype(jnp.float32)
    sigmoid = 1.0 / (1.0 + jnp.exp(-gate))
    silu = gate * sigmoid
    hidden = (silu * up).astype(bf16)
    gate_delta = (hidden_grad * up * sigmoid * (1.0 + gate * (1.0 - sigmoid))).astype(bf16)
    up_delta = (hidden_grad * silu).astype(bf16)
    partial = product(gate_delta, gate_weight, 1) + product(up_delta, up_weight, 1)
    input_grad = input_sum(partial.astype(bf16), inputs.shape[0])
    down_grad = product(hidden, all_grads, 0).astype(bf16)
    gate_grad = product(all_inputs, gate_delta, 0).astype(bf16)
    up_grad = product(all_inputs, up_delta, 0).astype(bf16)
    return input_grad, gate_grad, up_grad, down_grad


def solution(mesh):
    split = Mesh(mesh.devices.reshape(2, 2, 2, 2, 2, 2, 2, 2, 2), ROW + COL)
    tokens_by_col, tokens_by_row = P(COL, ROW), P(ROW, COL)
    in_specs = (
        tokens_by_col,
        tokens_by_col,
        tokens_by_row,
        tokens_by_row,
        tokens_by_row,
        tokens_by_row,
        tokens_by_col,
    )
    out_specs = (tokens_by_col, tokens_by_row, tokens_by_row, tokens_by_col)
    return jax.shard_map(
        per_device, mesh=split, in_specs=in_specs, out_specs=out_specs, check_vma=False
    )
```

time: 158 us -> 157 us (level)
  the two profiles are of different devices: /device:TPU:8 before, /device:TPU:2 now
where the time goes in v1:
time: 157 us; the launch traced here: 156 us
  starting transfers between devices  87.1 us (55%)
  waiting for transfers between devices  39.8 us (25%)
  other arithmetic  10.9 us (7%)
  local copies, waits for them, and re-layouts  8.4 us (5%)
  matrix products  5.95 us (4%)
  blocking collectives  2.3 us (1%)
    all_to_all x6, starting transfers between devices, exchanged(): return lax.all_to_all(blocks, axes, 0, 0, tiled=True)  44.1 us
    ppermute x9, starting transfers between devices, doubled(): other = lax.ppermute(array, axis, ((0, 1), (1, 0)))  43.1 us
    all_to_all x6, waiting for transfers between devices, exchanged(): return lax.all_to_all(blocks, axes, 0, 0, tiled=True)  25.3 us
    ppermute x9, waiting for transfers between devices, doubled(): other = lax.ppermute(array, axis, ((0, 1), (1, 0)))  14.5 us
    dot_general x6, matrix products, product(): lax.dot_general(x, y, (((contract,), (contract,)), ((), ())), preferred_e...  5.95 us
    another operation x17, other arithmetic, doubled(): jnp.stack((jnp.where(second, other, array), jnp.where(second, array, othe...  3.62 us
  transfers between devices with their start and end apart: 15, of which 5 were waited for; matrix products, arithmetic and copies ran while one was open for 11% of the time, Pallas kernels for 0%

profile of v1, /device:TPU:2, one launch (start us, length us, event | category | flops | bytes accessed | tf_op | source)
XLA Modules:
  0.0 155.6 jit_solution(17825686122114690678)
XLA Ops:
  0.7 1.4 broadcast_in_dim.6
  2.1 15.1 %all-to-all-start = ((bf16[8,16,512]{2,1,0:T(8,128)(2,1)}), bf16[8,16,512]{2,1,0:T(8,128)(2,1)S(1)}, u32[]{:S(2)}, u32[]{:S(2)}) async-start(bf16[8,16,512]{2,1,0:T(8,128)(2,1)} %broadcast_in_dim.6), calls=%async_computation | async-start | bytes 262144 | tf_op jit(solution)/shard_map/all_to_all | solution.py:21
  17.2 12.6 %collective-permute-start.4 = (bf16[16,512]{1,0:T(8,128)(2,1)}, bf16[16,512]{1,0:T(8,128)(2,1)S(1)}, u32[]{:S(2)}, u32[]{:S(2)}) collective-permute-start(bf16[16,512]{1,0:T(8,128)(2,1)} %param.7), channel_id=1, source_target_pairs={{0,8},{8,0},{1,9},{9,1},{2,10},{10,2},{3,11},{11,3},{4,12},{12,4},... | collective-permute-start | bytes 49160 | tf_op jit(solution)/shard_map/ppermute | solution.py:42
  29.8 0.8 pad_maximum_fusion.6
  30.6 5.1 %collective-permute-start = (bf16[2,32,512]{2,1,0:T(8,128)(2,1)S(1)}, bf16[2,32,512]{2,1,0:T(8,128)(2,1)S(1)}, u32[]{:S(2)}, u32[]{:S(2)}) collective-permute-start(bf16[2,32,512]{2,1,0:T(8,128)(2,1)S(1)} %pad_maximum_fusion.6), channel_id=1, source_target_pairs={{0,256},{256,0},{1,257},{257,1},{2,258},{258,2},{3,259},{259,3},{4... | collective-permute-start | bytes 196616 | tf_op jit(solution)/shard_map/ppermute | solution.py:42
  35.7 0.7 select_bitcast_fusion.17
  36.5 4.0 %collective-permute-start.5 = (bf16[2,16,512]{2,1,0:T(8,128)(2,1)S(1)}, bf16[2,16,512]{2,1,0:T(8,128)(2,1)S(1)}, u32[]{:S(2)}, u32[]{:S(2)}) collective-permute-start(bf16[2,16,512]{2,1,0:T(8,128)(2,1)S(1)} %pad_maximum_fusion.8), channel_id=1, source_target_pairs={{0,4},{4,0},{1,5},{5,1},{2,6},{6,2},{3,7},{7,3},{8,12},{12,8},{9,1... | collective-permute-start | bytes 98312 | tf_op jit(solution)/shard_map/ppermute | solution.py:42
  40.5 0.9 broadcast_in_dim.7
  41.3 3.5 %all-to-all-start.1 = ((bf16[4,8,16,512]{3,2,1,0:T(8,128)(2,1)}), bf16[4,8,16,512]{3,2,1,0:T(8,128)(2,1)S(1)}, u32[]{:S(2)}, u32[]{:S(2)}) async-start(bf16[4,8,16,512]{3,2,1,0:T(8,128)(2,1)} %broadcast_in_dim.7), calls=%async_computation.1 | async-start | bytes 1048576 | tf_op jit(solution)/shard_map/all_to_all | solution.py:21
  44.9 4.0 %collective-permute-start.1 = (bf16[2,2,32,512]{3,2,1,0:T(8,128)(2,1)S(1)}, bf16[2,2,32,512]{3,2,1,0:T(8,128)(2,1)S(1)}, u32[]{:S(2)}, u32[]{:S(2)}) collective-permute-start(bf16[2,2,32,512]{3,2,1,0:T(8,128)(2,1)S(1)} %pad_maximum_fusion.4), channel_id=1, source_target_pairs={{0,128},{128,0},{1,129},{129,1},{2,130},{130,2},{3,131},{131,3},{4... | collective-permute-start | bytes 393224 | tf_op jit(solution)/shard_map/ppermute | solution.py:42
  49.0 4.3 %collective-permute-start.6 = (bf16[2,2,16,512]{3,2,1,0:T(8,128)(2,1)S(1)}, bf16[2,2,16,512]{3,2,1,0:T(8,128)(2,1)S(1)}, u32[]{:S(2)}, u32[]{:S(2)}) collective-permute-start(bf16[2,2,16,512]{3,2,1,0:T(8,128)(2,1)S(1)} %pad_maximum_fusion.7), channel_id=1, source_target_pairs={{0,2},{2,0},{1,3},{3,1},{4,6},{6,4},{5,7},{7,5},{8,10},{10,8},{9,1... | collective-permute-start | bytes 196616 | tf_op jit(solution)/shard_map/ppermute | solution.py:42
  53.4 3.3 %collective-permute-start.2 = (bf16[2,2,2,32,512]{4,3,2,1,0:T(8,128)(2,1)S(1)}, bf16[2,2,2,32,512]{4,3,2,1,0:T(8,128)(2,1)S(1)}, u32[]{:S(2)}, u32[]{:S(2)}) collective-permute-start(bf16[2,2,2,32,512]{4,3,2,1,0:T(8,128)(2,1)S(1)} %pad_maximum_fusion.2), channel_id=1, source_target_pairs={{0,64},{64,0},{1,65},{65,1},{2,66},{66,2},{3,67},{67,3},{4,68},{68... | collective-permute-start | bytes 786440 | tf_op jit(solution)/shard_map/ppermute | solution.py:42
  56.8 4.9 %collective-permute-done.2 = bf16[2,2,2,32,512]{4,3,2,1,0:T(8,128)(2,1)S(1)} collective-permute-done((bf16[2,2,2,32,512]{4,3,2,1,0:T(8,128)(2,1)S(1)}, bf16[2,2,2,32,512]{4,3,2,1,0:T(8,128)(2,1)S(1)}, u32[]{:S(2)}, u32[]{:S(2)}) %collective-permute-start.2) | collective-permute-done | bytes 262176 | tf_op jit(solution)/shard_map/ppermute | solution.py:42
  61.8 1.9 %collective-permute-start.3 = (bf16[2,2,2,2,32,512]{5,4,3,2,1,0:T(8,128)(2,1)S(1)}, bf16[2,2,2,2,32,512]{5,4,3,2,1,0:T(8,128)(2,1)S(1)}, u32[]{:S(2)}, u32[]{:S(2)}) collective-permute-start(bf16[2,2,2,2,32,512]{5,4,3,2,1,0:T(8,128)(2,1)S(1)} %pad_maximum_fusion), channel_id=1, source_target_pairs={{0,32},{32,0},{1,33},{33,1},{2,34},{34,2},{3,35},{35,3},{4,36},{36... | collective-permute-start | bytes 1572872 | tf_op jit(solution)/shard_map/ppermute | solution.py:42
  63.7 3.9 %collective-permute-start.7 = (bf16[2,2,2,16,512]{4,3,2,1,0:T(8,128)(2,1)S(1)}, bf16[2,2,2,16,512]{4,3,2,1,0:T(8,128)(2,1)S(1)}, u32[]{:S(2)}, u32[]{:S(2)}) collective-permute-start(bf16[2,2,2,16,512]{4,3,2,1,0:T(8,128)(2,1)S(1)} %pad_maximum_fusion.5), channel_id=1, source_target_pairs={{0,1},{1,0},{2,3},{3,2},{4,5},{5,4},{6,7},{7,6},{8,9},{9,8},{10,11... | collective-permute-start | bytes 393224 | tf_op jit(solution)/shard_map/ppermute | solution.py:42
  67.7 0.8 copy-done.3
  68.4 1.3 convolution_convert_fusion.3
  69.7 7.4 %all-to-all-start.2 = ((bf16[16,32,512]{2,1,0:T(8,128)(2,1)}), bf16[16,32,512]{2,1,0:T(8,128)(2,1)S(1)}, u32[]{:S(2)}, u32[]{:S(2)}) async-start(bf16[16,32,512]{2,1,0:T(8,128)(2,1)} %bitcast.3), calls=%async_computation.2 | async-start | bytes 1048576 | tf_op jit(solution)/shard_map/all_to_all | solution.py:21
  77.2 1.5 maximum_convert_fusion
  78.7 7.0 %all-to-all-done.2 = bf16[16,32,512]{2,1,0:T(8,128)(2,1)S(1)} async-done(((bf16[16,32,512]{2,1,0:T(8,128)(2,1)}), bf16[16,32,512]{2,1,0:T(8,128)(2,1)S(1)}, u32[]{:S(2)}, u32[]{:S(2)}) %all-to-all-start.2) | async-done | bytes 524320 | tf_op jit(solution)/shard_map/all_to_all | solution.py:21
  85.8 0.7 broadcast_in_dim.8
  86.5 7.1 %all-to-all-start.3 = ((bf16[8,32,512]{2,1,0:T(8,128)(2,1)}), bf16[8,32,512]{2,1,0:T(8,128)(2,1)S(1)}, u32[]{:S(2)}, u32[]{:S(2)}) async-start(bf16[8,32,512]{2,1,0:T(8,128)(2,1)} %broadcast_in_dim.8), calls=%async_computation.3 | async-start | bytes 524288 | tf_op jit(solution)/shard_map/all_to_all | solution.py:21
  93.6 2.8 %fusion.21 = (f32[1,2,2,2,2,32,512]{6,5,4,3,2,1,0:T(8,128)}, f32[1,2,2,2,2,32,512]{6,5,4,3,2,1,0:T(8,128)S(1)}) fusion(f32[2,2,2,2,2,32,512]{6,5,4,3,2,1,0:T(8,128)} %maximum_convert_fusion), kind=kLoop, calls=%fused_computation.64 | loop fusion | bytes 4194304 | tf_op jit(solution)/shard_map/unstack | solution.py:86
  96.4 4.9 %all-to-all-done.3 = bf16[8,32,512]{2,1,0:T(8,128)(2,1)S(1)} async-done(((bf16[8,32,512]{2,1,0:T(8,128)(2,1)}), bf16[8,32,512]{2,1,0:T(8,128)(2,1)S(1)}, u32[]{:S(2)}, u32[]{:S(2)}) %all-to-all-start.3) | async-done | bytes 262176 | tf_op jit(solution)/shard_map/all_to_all | solution.py:21
  101.3 2.3 %all-gather = bf16[16,32,512]{2,1,0:T(8,128)(2,1)S(1)} all-gather(bf16[8,32,512]{2,1,0:T(8,128)(2,1)S(1)} %all-to-all-done.3), channel_id=2, replica_groups=mesh['y_hi'=2,'x_hi'=2,'x_lo'=2,'core'=2,'y_lo'=2,'z3'=2,'z2'=2,'z1'=2,'..., dimensions={0}, use_global_device_ids=true | all-gather | bytes 786432 | tf_op jit(solution)/shard_map/all_gather | solution.py:70
  103.6 0.1 convert_bitcast_fusion
  103.9 0.6 fusion.17
  104.5 0.4 copy-done.7
  104.9 0.5 fusion.22
  105.4 0.2 copy-done.5
  105.5 0.5 fusion
  106.0 0.8 copy.53
  106.8 4.1 %all-to-all-start.4 = ((bf16[4,8,16,512]{3,2,1,0:T(8,128)(2,1)}), bf16[4,8,16,512]{3,2,1,0:T(8,128)(2,1)}, u32[]{:S(2)}, u32[]{:S(2)}) async-start(bf16[4,8,16,512]{3,2,1,0:T(8,128)(2,1)} %bitcast.160), calls=%async_computation.4 | async-start | bytes 1048576 | tf_op jit(solution)/shard_map/all_to_all | solution.py:21
  111.0 0.7 pad_maximum_fusion.3
  111.7 3.9 %collective-permute-start.8 = (bf16[2,2,2,2,16,512]{5,4,3,2,1,0:T(8,128)(2,1)}, bf16[2,2,2,2,16,512]{5,4,3,2,1,0:T(8,128)(2,1)}, u32[]{:S(2)}, u32[]{:S(2)}) collective-permute-start(bf16[2,2,2,2,16,512]{5,4,3,2,1,0:T(8,128)(2,1)} %pad_maximum_fusion.3), channel_id=1, source_target_pairs={{0,16},{16,0},{1,17},{17,1},{2,18},{18,2},{3,19},{19,3},{4,20},{20... | collective-permute-start | bytes 786440 | tf_op jit(solution)/shard_map/ppermute | solution.py:42
  115.6 9.6 %collective-permute-done.8 = bf16[2,2,2,2,16,512]{5,4,3,2,1,0:T(8,128)(2,1)} collective-permute-done((bf16[2,2,2,2,16,512]{5,4,3,2,1,0:T(8,128)(2,1)}, bf16[2,2,2,2,16,512]{5,4,3,2,1,0:T(8,128)(2,1)}, u32[]{:S(2)}, u32[]{:S(2)}) %collective-permute-start.8) | collective-permute-done | bytes 262176 | tf_op jit(solution)/shard_map/ppermute | solution.py:42
  125.2 1.0 select_bitcast_fusion.3
  126.2 0.8 pad_maximum_fusion.1
  127.1 0.3 multiply_convert_fusion
  127.5 0.2 copy-done.2
  127.6 1.4 fusion.8
  129.1 1.3 convolution_convert_fusion
  130.3 1.8 %reduce_sum.37 = bf16[8,16,512]{2,1,0:T(8,128)(2,1)} reduce(bf16[4,8,16,512]{3,2,1,0:T(8,128)(2,1)} %all-to-all-done.4, bf16[]{:T(256)} %constant.32.clone.1), dimensions={0}, to_apply=%region_1.2 | reduce | flops 196608 | bytes 655362 | tf_op jit(solution)/shard_map/reduce_sum | solution.py:30
  132.1 6.9 %all-to-all-start.5 = ((bf16[8,16,512]{2,1,0:T(8,128)(2,1)}), bf16[8,16,512]{2,1,0:T(8,128)(2,1)S(1)}, u32[]{:S(2)}, u32[]{:S(2)}) async-start(bf16[8,16,512]{2,1,0:T(8,128)(2,1)} %reduce_sum.37), calls=%async_computation.5 | async-start | bytes 262144 | tf_op jit(solution)/shard_map/all_to_all | solution.py:21
  139.0 1.3 convolution_convert_fusion.1
  140.3 1.3 convolution_convert_fusion.2
  141.5 13.4 %all-to-all-done.5 = bf16[8,16,512]{2,1,0:T(8,128)(2,1)S(1)} async-done(((bf16[8,16,512]{2,1,0:T(8,128)(2,1)}), bf16[8,16,512]{2,1,0:T(8,128)(2,1)S(1)}, u32[]{:S(2)}, u32[]{:S(2)}) %all-to-all-start.5) | async-done | bytes 131104 | tf_op jit(solution)/shard_map/all_to_all | solution.py:21
  154.9 0.6 reduce_sum.38
  (45 shorter events, 0.7 us)
Async XLA Ops:
  0.6 67.8 %copy-start = (bf16[512,512]{1,0:T(8,128)(2,1)S(1)}, bf16[512,512]{1,0:T(8,128)(2,1)}, u32[]{:S(2)}) copy-start(bf16[512,512]{1,0:T(8,128)(2,1)} %param.13) | copy-start | bytes 1572868
  0.6 44.2 %copy-start.10 = (bf16[32,512]{1,0:T(8,128)(2,1)S(1)}, bf16[32,512]{1,0:T(8,128)(2,1)}, u32[]{:S(2)}) copy-start(bf16[32,512]{1,0:T(8,128)(2,1)} %param.9) | copy-start | bytes 98308
  0.7 44.2 %copy-start.9 = (bf16[32,512]{1,0:T(8,128)(2,1)S(1)}, bf16[32,512]{1,0:T(8,128)(2,1)}, u32[]{:S(2)}) copy-start(bf16[32,512]{1,0:T(8,128)(2,1)} %param.10) | copy-start | bytes 98308
  2.1 38.4 %all-to-all-start = ((bf16[8,16,512]{2,1,0:T(8,128)(2,1)}), bf16[8,16,512]{2,1,0:T(8,128)(2,1)S(1)}, u32[]{:S(2)}, u32[]{:S(2)}) async-start(bf16[8,16,512]{2,1,0:T(8,128)(2,1)} %broadcast_in_dim.6), calls=%async_computation | async-start | bytes 262144 | tf_op jit(solution)/shard_map/all_to_all | solution.py:21
  17.2 18.5 %collective-permute-start.4 = (bf16[16,512]{1,0:T(8,128)(2,1)}, bf16[16,512]{1,0:T(8,128)(2,1)S(1)}, u32[]{:S(2)}, u32[]{:S(2)}) collective-permute-start(bf16[16,512]{1,0:T(8,128)(2,1)} %param.7), channel_id=1, source_target_pairs={{0,8},{8,0},{1,9},{9,1},{2,10},{10,2},{3,11},{11,3},{4,12},{12,4},... | collective-permute-start | bytes 49160 | tf_op jit(solution)/shard_map/ppermute | solution.py:42
  30.6 14.2 %collective-permute-start = (bf16[2,32,512]{2,1,0:T(8,128)(2,1)S(1)}, bf16[2,32,512]{2,1,0:T(8,128)(2,1)S(1)}, u32[]{:S(2)}, u32[]{:S(2)}) collective-permute-start(bf16[2,32,512]{2,1,0:T(8,128)(2,1)S(1)} %pad_maximum_fusion.6), channel_id=1, source_target_pairs={{0,256},{256,0},{1,257},{257,1},{2,258},{258,2},{3,259},{259,3},{4... | collective-permute-start | bytes 196616 | tf_op jit(solution)/shard_map/ppermute | solution.py:42
  36.5 12.4 %collective-permute-start.5 = (bf16[2,16,512]{2,1,0:T(8,128)(2,1)S(1)}, bf16[2,16,512]{2,1,0:T(8,128)(2,1)S(1)}, u32[]{:S(2)}, u32[]{:S(2)}) collective-permute-start(bf16[2,16,512]{2,1,0:T(8,128)(2,1)S(1)} %pad_maximum_fusion.8), channel_id=1, source_target_pairs={{0,4},{4,0},{1,5},{5,1},{2,6},{6,2},{3,7},{7,3},{8,12},{12,8},{9,1... | collective-permute-start | bytes 98312 | tf_op jit(solution)/shard_map/ppermute | solution.py:42
  41.3 26.3 %all-to-all-start.1 = ((bf16[4,8,16,512]{3,2,1,0:T(8,128)(2,1)}), bf16[4,8,16,512]{3,2,1,0:T(8,128)(2,1)S(1)}, u32[]{:S(2)}, u32[]{:S(2)}) async-start(bf16[4,8,16,512]{3,2,1,0:T(8,128)(2,1)} %broadcast_in_dim.7), calls=%async_computation.1 | async-start | bytes 1048576 | tf_op jit(solution)/shard_map/all_to_all | solution.py:21
  44.9 8.4 %collective-permute-start.1 = (bf16[2,2,32,512]{3,2,1,0:T(8,128)(2,1)S(1)}, bf16[2,2,32,512]{3,2,1,0:T(8,128)(2,1)S(1)}, u32[]{:S(2)}, u32[]{:S(2)}) collective-permute-start(bf16[2,2,32,512]{3,2,1,0:T(8,128)(2,1)S(1)} %pad_maximum_fusion.4), channel_id=1, source_target_pairs={{0,128},{128,0},{1,129},{129,1},{2,130},{130,2},{3,131},{131,3},{4... | collective-permute-start | bytes 393224 | tf_op jit(solution)/shard_map/ppermute | solution.py:42
  49.0 7.8 %collective-permute-start.6 = (bf16[2,2,16,512]{3,2,1,0:T(8,128)(2,1)S(1)}, bf16[2,2,16,512]{3,2,1,0:T(8,128)(2,1)S(1)}, u32[]{:S(2)}, u32[]{:S(2)}) collective-permute-start(bf16[2,2,16,512]{3,2,1,0:T(8,128)(2,1)S(1)} %pad_maximum_fusion.7), channel_id=1, source_target_pairs={{0,2},{2,0},{1,3},{3,1},{4,6},{6,4},{5,7},{7,5},{8,10},{10,8},{9,1... | collective-permute-start | bytes 196616 | tf_op jit(solution)/shard_map/ppermute | solution.py:42
  53.4 8.3 %collective-permute-start.2 = (bf16[2,2,2,32,512]{4,3,2,1,0:T(8,128)(2,1)S(1)}, bf16[2,2,2,32,512]{4,3,2,1,0:T(8,128)(2,1)S(1)}, u32[]{:S(2)}, u32[]{:S(2)}) collective-permute-start(bf16[2,2,2,32,512]{4,3,2,1,0:T(8,128)(2,1)S(1)} %pad_maximum_fusion.2), channel_id=1, source_target_pairs={{0,64},{64,0},{1,65},{65,1},{2,66},{66,2},{3,67},{67,3},{4,68},{68... | collective-permute-start | bytes 786440 | tf_op jit(solution)/shard_map/ppermute | solution.py:42
  61.8 15.4 %collective-permute-start.3 = (bf16[2,2,2,2,32,512]{5,4,3,2,1,0:T(8,128)(2,1)S(1)}, bf16[2,2,2,2,32,512]{5,4,3,2,1,0:T(8,128)(2,1)S(1)}, u32[]{:S(2)}, u32[]{:S(2)}) collective-permute-start(bf16[2,2,2,2,32,512]{5,4,3,2,1,0:T(8,128)(2,1)S(1)} %pad_maximum_fusion), channel_id=1, source_target_pairs={{0,32},{32,0},{1,33},{33,1},{2,34},{34,2},{3,35},{35,3},{4,36},{36... | collective-permute-start | bytes 1572872 | tf_op jit(solution)/shard_map/ppermute | solution.py:42
  63.7 13.4 %collective-permute-start.7 = (bf16[2,2,2,16,512]{4,3,2,1,0:T(8,128)(2,1)S(1)}, bf16[2,2,2,16,512]{4,3,2,1,0:T(8,128)(2,1)S(1)}, u32[]{:S(2)}, u32[]{:S(2)}) collective-permute-start(bf16[2,2,2,16,512]{4,3,2,1,0:T(8,128)(2,1)S(1)} %pad_maximum_fusion.5), channel_id=1, source_target_pairs={{0,1},{1,0},{2,3},{3,2},{4,5},{5,4},{6,7},{7,6},{8,9},{9,8},{10,11... | collective-permute-start | bytes 393224 | tf_op jit(solution)/shard_map/ppermute | solution.py:42
  67.7 0.8 copy-start.3
  69.7 16.0 %all-to-all-start.2 = ((bf16[16,32,512]{2,1,0:T(8,128)(2,1)}), bf16[16,32,512]{2,1,0:T(8,128)(2,1)S(1)}, u32[]{:S(2)}, u32[]{:S(2)}) async-start(bf16[16,32,512]{2,1,0:T(8,128)(2,1)} %bitcast.3), calls=%async_computation.2 | async-start | bytes 1048576 | tf_op jit(solution)/shard_map/all_to_all | solution.py:21
  86.5 14.8 %all-to-all-start.3 = ((bf16[8,32,512]{2,1,0:T(8,128)(2,1)}), bf16[8,32,512]{2,1,0:T(8,128)(2,1)S(1)}, u32[]{:S(2)}, u32[]{:S(2)}) async-start(bf16[8,32,512]{2,1,0:T(8,128)(2,1)} %broadcast_in_dim.8), calls=%async_computation.3 | async-start | bytes 524288 | tf_op jit(solution)/shard_map/all_to_all | solution.py:21
  101.3 2.5 %copy-start.1 = (f32[1,2,2,2,2,32,512]{6,5,4,3,2,1,0:T(8,128)S(1)}, f32[1,2,2,2,2,32,512]{6,5,4,3,2,1,0:T(8,128)}, u32[]{:S(2)}) copy-start(f32[1,2,2,2,2,32,512]{6,5,4,3,2,1,0:T(8,128)} %get-tuple-element.8) | copy-start | bytes 3145732
  103.9 1.0 copy-start.7
  104.4 1.1 copy-start.5
  106.8 23.5 %all-to-all-start.4 = ((bf16[4,8,16,512]{3,2,1,0:T(8,128)(2,1)}), bf16[4,8,16,512]{3,2,1,0:T(8,128)(2,1)}, u32[]{:S(2)}, u32[]{:S(2)}) async-start(bf16[4,8,16,512]{3,2,1,0:T(8,128)(2,1)} %bitcast.160), calls=%async_computation.4 | async-start | bytes 1048576 | tf_op jit(solution)/shard_map/all_to_all | solution.py:21
  111.7 13.5 %collective-permute-start.8 = (bf16[2,2,2,2,16,512]{5,4,3,2,1,0:T(8,128)(2,1)}, bf16[2,2,2,2,16,512]{5,4,3,2,1,0:T(8,128)(2,1)}, u32[]{:S(2)}, u32[]{:S(2)}) collective-permute-start(bf16[2,2,2,2,16,512]{5,4,3,2,1,0:T(8,128)(2,1)} %pad_maximum_fusion.3), channel_id=1, source_target_pairs={{0,16},{16,0},{1,17},{17,1},{2,18},{18,2},{3,19},{19,3},{4,20},{20... | collective-permute-start | bytes 786440 | tf_op jit(solution)/shard_map/ppermute | solution.py:42
  126.2 1.4 copy-start.2
  127.6 1.4 copy-start.4
  129.1 9.9 %copy-start.6 = (bf16[2,2,2,2,2,16,512]{6,5,4,3,2,1,0:T(8,128)(2,1)S(1)}, bf16[2,2,2,2,2,16,512]{6,5,4,3,2,1,0:T(8,128)(2,1)}, u32[]{:S(2)}) copy-start(bf16[2,2,2,2,2,16,512]{6,5,4,3,2,1,0:T(8,128)(2,1)} %pad_maximum_fusion.1) | copy-start | bytes 1572868
  129.1 11.2 %copy-start.8 = (bf16[1,512,512]{2,1,0:T(8,128)(2,1)S(1)}, bf16[1,512,512]{2,1,0:T(8,128)(2,1)}, u32[]{:S(2)}) copy-start(bf16[1,512,512]{2,1,0:T(8,128)(2,1)} %get-tuple-element.5) | copy-start | bytes 1572868
  132.1 22.8 %all-to-all-start.5 = ((bf16[8,16,512]{2,1,0:T(8,128)(2,1)}), bf16[8,16,512]{2,1,0:T(8,128)(2,1)S(1)}, u32[]{:S(2)}, u32[]{:S(2)}) async-start(bf16[8,16,512]{2,1,0:T(8,128)(2,1)} %reduce_sum.37), calls=%async_computation.5 | async-start | bytes 262144 | tf_op jit(solution)/shard_map/all_to_all | solution.py:21
